TPU v7x, 32 devices: a whole 2x2x4 slice. The times are simulated.
32 devices in a mesh: frames: 4 (over y, core), win: 8 (over z, x).
Axes of the slice: x: 2, y: 2, z: 4, core: 2. Of those that a mesh axis runs over, the one named last changes fastest.
Arguments:
- memberships: float32 [8, 256, 4096], P('win', 'frames'), as said below
- lag_times: int32 [8], P('win'), may hold values from 1 to 8, as said below
- segment_ids: int32 [8, 256], P('win'), may hold values from 0 to 7, never falling along the last dimension, each value on 1 to 128 neighbouring positions
- bias_codes: int32 [8, 4096], P('win'), may hold values from 0 to 511
Outputs:
- free_energy: float32 [4096], P('frames')
- log_multipliers: float32 [8, 4096], P('win', 'frames')
Inputs may be any that keep to these rules, and one draw needn't show every extreme that they name: Positive; each frame's memberships sum to one up to rounding. `lag_times`: some window's lag time is 8.
All inputs are finite; a program needn't handle non-finite values.
Results may differ from a plain program's by a relative error of at most 0.00041.
Values may be sent and summed in bfloat16 or wider, within the bound.
No kernel may reach another device: no remote copies, remote signals or barrier semaphores. Data moves between devices by JAX's collectives and lax.ppermute only.
A program may use at most 64 MiB of HBM per device.

v0:
```python
import jax
import jax.numpy as jnp
from jax import lax
from jax.sharding import PartitionSpec as P

LAGMAX = 8
ITERS = 2
bias_unit = 1.0 / 128.0


def shifted(block, axis, distance):
    devices = range(lax.axis_size(axis))
    route = [(i - distance, i) for i in devices if i - distance in devices]
    return lax.ppermute(block, axis, route)


def split_rows(block, frames_dev, lag_time, valid_all):
    width = frames_dev + LAGMAX
    number = block.shape[0] // width
    states = block.shape[1]
    shaped = block.reshape(number, width, states)
    current = shaped[:, :frames_dev].reshape(number * frames_dev, states)
    later = lax.dynamic_slice_in_dim(shaped, lag_time, frames_dev, 1).reshape(
        number * frames_dev, states
    )
    later = jnp.where(valid_all[:, None], later, jnp.zeros((), later.dtype))
    return (current, later)


def add_pair(accumulated, current, later, first, rows):
    current_cols = lax.dynamic_slice_in_dim(current, first, rows, 1)
    later_cols = lax.dynamic_slice_in_dim(later, first, rows, 1)
    accumulated = jnp.einsum("tr,ts->rs", current_cols, later, preferred_element_type=jnp.float32)
    return accumulated + jnp.einsum(
        "tr,ts->rs", later_cols, current, preferred_element_type=jnp.float32
    )


def shards(memberships, lag_times, segment_ids, bias_codes):
    member = memberships[0].astype(jnp.bfloat16)
    lag_time = lag_times[0]
    segment_row = segment_ids[0]
    frames_dev = member.shape[0]
    states = member.shape[1]
    frames_all = segment_row.shape[0]
    rows = states // lax.axis_size("frames")
    position = lax.axis_index("frames")
    first = position * rows
    heading = shifted(member[:LAGMAX], "frames", -1)
    extended = jnp.concatenate([member, heading], axis=0)
    segment_ext = jnp.concatenate([segment_row, jnp.full((LAGMAX,), -1, jnp.int32)])
    valid_all = segment_row == lax.dynamic_slice_in_dim(segment_ext, lag_time, frames_all, 0)
    empty = jnp.zeros((rows, states), jnp.float32)
    current, later = split_rows(
        lax.all_gather(extended, "frames", axis=0, tiled=True), frames_dev, lag_time, valid_all
    )
    sym_counts = add_pair(empty, current, later, first, rows)
    gammas = jnp.exp(-bias_codes[0].astype(jnp.float32) * bias_unit)
    gamma_rows = lax.dynamic_slice_in_dim(gammas, first, rows, 0)
    mult_rows = jnp.sum(sym_counts, axis=1) * 0.5
    mult_full = lax.all_gather(mult_rows, "frames", axis=0, tiled=True)
    window_total = jnp.sum(mult_full)
    count_rows = lax.psum(mult_rows, "win")
    weights = jnp.full((states,), 1.0 / states, jnp.float32)
    for sweep in range(ITERS):
        scaled = gammas * weights
        scaled_rows = lax.dynamic_slice_in_dim(scaled, first, rows, 0)
        denom = mult_rows[:, None] * scaled[None, :] + scaled_rows[:, None] * mult_full[None, :]
        ratios = sym_counts / denom
        new_rows = mult_rows * jnp.sum(ratios * scaled[None, :], axis=1)
        terms = gamma_rows * jnp.sum(ratios * mult_full[None, :], axis=1)
        term_rows = lax.psum(terms, "win")
        raw_rows = count_rows / term_rows
        if sweep + 1 < ITERS:
            raw_full, mult_full = (
                lax.all_gather(raw_rows, "frames", axis=0, tiled=True),
                lax.all_gather(new_rows, "frames", axis=0, tiled=True),
            )
        else:
            raw_full = lax.all_gather(raw_rows, "frames", axis=0, tiled=True)
        weights = raw_full / jnp.sum(raw_full)
        mult_rows = new_rows
    weight_rows = lax.dynamic_slice_in_dim(weights, first, rows, 0)
    free_energy = -jnp.log(states * weight_rows)
    log_multipliers = jnp.log(mult_rows * states / window_total)[None, :]
    return (free_energy, log_multipliers)


def solution(mesh):
    placed = (P("win", "frames", None), P("win"), P("win", None), P("win", None))
    return jax.shard_map(
        shards,
        mesh=mesh,
        in_specs=placed,
        out_specs=(P("frames"), P("win", "frames")),
        check_vma=False,
    )
```

profile of v0, /device:TPU:0, one launch (start us, length us, event | category | flops | bytes accessed | tf_op | source)
XLA Modules:
  0.0 147.7 jit_solution(16507466639481832255)
XLA Ops:
  7.2 0.0 all-gather.2.cloned.1.call-start
  7.2 1.3 convert_element_type.11
  8.5 1.3 collective-permute-start
  9.8 1.3 convert_bitcast_fusion
  11.1 0.6 collective-permute-done
  11.7 0.9 pad_maximum_fusion
  12.5 0.0 all-gather.2.cloned.1.call-update
  13.2 0.8 broadcast_multiply_fusion
  14.0 0.8 fusion.6
  14.8 25.7 %all-gather.2.cloned.1.call-done = bf16[288,4096]{1,0:T(8,128)(2,1)} async-done(((bf16[72,4096]{1,0:T(8,128)(2,1)}), bf16[288,4096]{1,0:T(8,128)(2,1)}) %all-gather.2.cloned.1.call-update) | async-done | bytes 2359312 | tf_op jit(solution)/shard_map/all_gather | solution.py:55
  40.5 2.9 %fusion.10 = (bf16[4,64,4096]{2,1,0:T(8,128)(2,1)S(1)}, bf16[4,64,4096]{2,1,0:T(8,128)(2,1)S(1)}) fusion(bf16[4,72,4096]{2,1,0:T(8,128)(2,1)} %bitcast.23, s32[]{:T(128)S(6)} %select_n.20), kind=kLoop, calls=%fused_computation.30 | loop fusion | bytes 8388612 | tf_op jit(solution)/shard_map/slice | solution.py:22
  43.4 0.0 copy-start.1
  43.4 0.4 bitcast_select_fusion
  43.8 0.9 copy-done.1
  44.8 8.1 %fusion.1 = f32[1024,4096]{1,0:T(8,128)} fusion(bf16[256,4096]{1,0:T(8,128)(2,1)S(1)} %bitcast_select_fusion, bf16[256,4096]{1,0:T(8,128)(2,1)S(1)} %bitcast.21, s32[]{:T(128)S(6)} %select_n.18), kind=kOutput, calls=%fused_computation.10 | convolution fusion | flops 2147483648 | bytes 19398660 | tf_op jit(solution)/shard_map/tr,ts->rs/dot_general | solution.py:33
  52.9 7.8 %fusion.11 = (f32[1024]{0:T(1024)S(1)}, f32[1024,4096]{1,0:T(8,128)S(1)}) fusion(f32[1024,4096]{1,0:T(8,128)} %fusion.1, bf16[256,4096]{1,0:T(8,128)(2,1)} %bitcast.22, bf16[256,4096]{1,0:T(8,128)(2,1)S(1)} %bitcast_select_fusion, s32[]{:T(128)S(6)} %select_n.18), kind=kOutput, calls=%fused_computation.31 | convolution fusion | flops 2155871232 | bytes 36179972 | tf_op jit(solution)/shard_map/tr,ts->rs/dot_general | solution.py:34
  60.7 0.0 copy-start
  60.7 5.2 %all_gather.16 = f32[4096]{0:T(1024)S(1)} all-gather(f32[1024]{0:T(1024)S(1)} %broadcast_multiply_fusion.1), channel_id=1, replica_groups=mesh['frames'=4,'win'=8] {'frames'}, dimensions={0}, use_global_device_ids=true | all-gather | bytes 20480 | tf_op jit(solution)/shard_map/all_gather | solution.py:61
  65.9 0.5 copy-done
  66.4 6.2 %multiply_reduce_fusion.2 = (f32[1024]{0:T(1024)S(1)}, f32[1024]{0:T(1024)S(1)}) fusion(f32[4096]{0:T(1024)S(1)} %all_gather.16, f32[4096]{0:T(1024)S(1)} %bitcast.26, f32[1024,4096]{1,0:T(8,128)S(1)} %get-tuple-element.13, f32[1024]{0:T(1024)S(1)} %dynamic-slice_multiply_fusion, f32[1024]{0:T(1024)S(1)} %broadcast_multiply_fusion.1), kind=kLoop, calls=%fused_computation.3 | loop fusion | flops 33552384 | bytes 16826368 | tf_op jit(solution)/shard_map/reduce_sum | solution.py:71
  72.6 5.2 %all_gather.18 = f32[4096]{0:T(1024)S(1)} all-gather(f32[1024]{0:T(1024)S(1)} %fusion.9), channel_id=1, replica_groups=mesh['frames'=4,'win'=8] {'frames'}, dimensions={0}, use_global_device_ids=true | all-gather | bytes 20480 | tf_op jit(solution)/shard_map/all_gather | solution.py:77
  77.8 21.6 %all-reduce.1 = (f32[1024]{0:T(1024)S(1)}, f32[1024]{0:T(1024)S(1)}) all-reduce(f32[1024]{0:T(1024)S(1)} %broadcast_multiply_fusion.1, f32[1024]{0:T(1024)S(1)} %mul.185), channel_id=1, replica_groups=mesh['frames'=4,'win'=8] {'win'}, use_global_device_ids=true, to_apply=%region_1.2 | all-reduce | flops 2048 | bytes 16384 | tf_op jit(solution)/shard_map/psum | solution.py:63
  99.4 5.2 %all_gather.17 = f32[4096]{0:T(1024)S(1)} all-gather(f32[1024]{0:T(1024)S(1)} %div.38), channel_id=1, replica_groups=mesh['frames'=4,'win'=8] {'frames'}, dimensions={0}, use_global_device_ids=true | all-gather | bytes 20480 | tf_op jit(solution)/shard_map/all_gather | solution.py:76
  104.6 0.6 reduce_sum.79
  105.2 0.6 reduce_sum.75
  105.8 0.7 divide_multiply_fusion
  106.5 9.0 %multiply_reduce_fusion = (f32[1024]{0:T(1024)S(1)}, f32[1024]{0:T(1024)S(1)}) fusion(f32[4096]{0:T(1024)S(1)} %divide_multiply_fusion, f32[4096]{0:T(1024)S(1)} %all_gather.18, f32[1024,4096]{1,0:T(8,128)} %copy-done, f32[1024]{0:T(1024)S(1)} %dynamic_slice.33, f32[1024]{0:T(1024)S(1)} %fusion.9), kind=kLoop, calls=%fused_computation | loop fusion | flops 33552384 | bytes 16826368 | tf_op jit(solution)/shard_map/reduce_sum | solution.py:70
  115.5 17.1 %psum.23 = f32[1024]{0:T(1024)S(1)} all-reduce(f32[1024]{0:T(1024)S(1)} %mul.193), channel_id=1, replica_groups=mesh['frames'=4,'win'=8] {'win'}, use_global_device_ids=true, to_apply=%region_7.8 | all-reduce | flops 1024 | bytes 8192 | tf_op jit(solution)/shard_map/psum | solution.py:72
  132.7 5.2 %all_gather.19 = f32[4096]{0:T(1024)S(1)} all-gather(f32[1024]{0:T(1024)S(1)} %div.42), channel_id=1, replica_groups=mesh['frames'=4,'win'=8] {'frames'}, dimensions={0}, use_global_device_ids=true | all-gather | bytes 20480 | tf_op jit(solution)/shard_map/all_gather | solution.py:80
  137.9 0.6 reduce_sum.77
  138.5 1.3 fusion.5
  139.7 1.2 divide_log_fusion
  (10 shorter events, 0.1 us)
Async XLA Ops:
  7.2 33.3 %all-gather.2.cloned.1.call-start = ((), (), s32[]{:S(2)}) async-start(), calls=%async_computation | async-start | bytes 2949120 | tf_op jit(solution)/shard_map/all_gather | solution.py:55
  8.5 3.1 %collective-permute-start = (bf16[8,4096]{1,0:T(8,128)(2,1)S(1)}, bf16[8,4096]{1,0:T(8,128)(2,1)S(1)}, u32[]{:S(2)}, u32[]{:S(2)}) collective-permute-start(bf16[8,4096]{1,0:T(8,128)(2,1)S(1)} %slice_bitcast_fusion), channel_id=1, source_target_pairs={{8,0},{16,8},{24,16},{9,1},{17,9},{25,17},{10,2},{18,10},{26,18},{... | collective-permute-start | bytes 196616 | tf_op jit(solution)/shard_map/ppermute | solution.py:14
  43.4 1.4 copy-start.1
  60.7 5.7 %copy-start = (f32[1024,4096]{1,0:T(8,128)}, f32[1024,4096]{1,0:T(8,128)S(1)}, u32[]{:S(2)}) copy-start(f32[1024,4096]{1,0:T(8,128)S(1)} %get-tuple-element.13) | copy-start | bytes 50331652
Sparse Core Ops, SparseCore 0:
  12.7 27.7 all-gather.1
where the time goes:
time: 148 us
  blocking collectives  59.6 us (40%)
  waiting for transfers between devices  26.2 us (18%)
  other arithmetic  25.5 us (17%)
  matrix products  15.9 us (11%)
  between operations  14.8 us (10%)
  local copies, waits for them, and re-layouts  4.38 us (3%)
    all_gather x1, waiting for transfers between devices, shards(): lax.all_gather(extended, 'frames', axis=0, tiled=True)  25.7 us
    psum x1, blocking collectives, shards(): count_rows = lax.psum(mult_rows, 'win')  21.6 us
    psum x1, blocking collectives, shards(): term_rows = lax.psum(terms, 'win')  17.1 us
    reduce_sum x1, other arithmetic, shards(): new_rows = mult_rows * jnp.sum(ratios * scaled[None, :], axis=1)  8.98 us
    dot_general x1, matrix products, add_pair(): jnp.einsum('tr,ts->rs', current_cols, later, preferred_element_type=jnp.f...  8.12 us
    dot_general x1, matrix products, add_pair(): jnp.einsum('tr,ts->rs', later_cols, current, preferred_element_type=jnp.f...  7.76 us
    reduce_sum x1, other arithmetic, shards(): terms = gamma_rows * jnp.sum(ratios * mult_full[None, :], axis=1)  6.19 us
    all_gather x1, blocking collectives, shards(): mult_full = lax.all_gather(mult_rows, 'frames', axis=0, tiled=True)  5.21 us
  transfers between devices with their start and end apart: 2, of which 2 were waited for; matrix products, arithmetic and copies ran while one was open for 2% of the time, Pallas kernels for 0%

commit v1 on v0

--- a/solution.py
+++ b/solution.py
@@ -69,7 +69,7 @@
         ratios = sym_counts / denom
         new_rows = mult_rows * jnp.sum(ratios * scaled[None, :], axis=1)
         terms = gamma_rows * jnp.sum(ratios * mult_full[None, :], axis=1)
-        term_rows = lax.psum(terms, "win")
+        term_rows = jnp.sum(lax.all_gather(terms, "win"), axis=0)
         raw_rows = count_rows / term_rows
         if sweep + 1 < ITERS:
             raw_full, mult_full = (

time: 148 us -> 190 us (1.28)
  blocking collectives: 59.6 us -> 103 us
  matrix products: 15.9 us -> 11.2 us
  other arithmetic: 25.5 us -> 28.5 us
    all_gather x0 -> x2, blocking collectives: none -> 61.2 us  [shards(): term_rows = jnp.sum(lax.all_gather(terms, 'win'), axis=0)]
    psum x1 -> x0, blocking collectives: 17.1 us -> none  [shards(): term_rows = lax.psum(terms, 'win')]
    dot_general x1, matrix products: 8.12 us -> 2.41 us  [add_pair(): jnp.einsum('tr,ts->rs', current_cols, later, preferred_element_type=jnp.f...]
    reduce_sum x1, other arithmetic: 6.19 us -> 9.14 us  [shards(): terms = gamma_rows * jnp.sum(ratios * mult_full[None, :], axis=1)]
where the time goes in v1:
time: 190 us; the launch traced here: 189 us
  blocking collectives  103 us (54%)
  other arithmetic  28.5 us (15%)
  waiting for transfers between devices  26.2 us (14%)
  between operations  14.8 us (8%)
  matrix products  11.2 us (6%)
  local copies, waits for them, and re-layouts  3.92 us (2%)
    all_gather x2, blocking collectives, shards(): term_rows = jnp.sum(lax.all_gather(terms, 'win'), axis=0)  61.2 us
    all_gather x1, waiting for transfers between devices, shards(): lax.all_gather(extended, 'frames', axis=0, tiled=True)  25.7 us
    psum x1, blocking collectives, shards(): count_rows = lax.psum(mult_rows, 'win')  21.3 us
    reduce_sum x1, other arithmetic, shards(): terms = gamma_rows * jnp.sum(ratios * mult_full[None, :], axis=1)  9.14 us
    reduce_sum x1, other arithmetic, shards(): new_rows = mult_rows * jnp.sum(ratios * scaled[None, :], axis=1)  8.99 us
    dot_general x1, matrix products, add_pair(): jnp.einsum('tr,ts->rs', later_cols, current, preferred_element_type=jnp.f...  8.77 us
    all_gather x1, blocking collectives, shards(): lax.all_gather(new_rows, 'frames', axis=0, tiled=True)  5.21 us
    all_gather x1, blocking collectives, shards(): lax.all_gather(raw_rows, 'frames', axis=0, tiled=True)  5.21 us
  transfers between devices with their start and end apart: 2, of which 2 were waited for; matrix products, arithmetic and copies ran while one was open for 2% of the time, Pallas kernels for 0%

profile of v1, /device:TPU:0, one launch (start us, length us, event | category | flops | bytes accessed | tf_op | source)
XLA Modules:
  0.0 189.3 jit_solution(8113734344410783831)
XLA Ops:
  7.2 0.0 all-gather.4.cloned.1.call-start
  7.2 1.3 convert_element_type.11
  8.5 1.3 collective-permute-start
  9.8 1.3 convert_bitcast_fusion
  11.1 0.6 collective-permute-done
  11.7 0.9 pad_maximum_fusion
  12.5 0.0 all-gather.4.cloned.1.call-update
  13.2 0.8 broadcast_multiply_fusion
  14.0 0.8 fusion.6
  14.8 25.7 %all-gather.4.cloned.1.call-done = bf16[288,4096]{1,0:T(8,128)(2,1)} async-done(((bf16[72,4096]{1,0:T(8,128)(2,1)}), bf16[288,4096]{1,0:T(8,128)(2,1)}) %all-gather.4.cloned.1.call-update) | async-done | bytes 2359312 | tf_op jit(solution)/shard_map/all_gather | solution.py:55
  40.5 2.9 %fusion.10 = (bf16[4,64,4096]{2,1,0:T(8,128)(2,1)S(1)}, bf16[4,64,4096]{2,1,0:T(8,128)(2,1)S(1)}) fusion(bf16[4,72,4096]{2,1,0:T(8,128)(2,1)} %bitcast.23, s32[]{:T(128)S(6)} %select_n.20), kind=kLoop, calls=%fused_computation.30 | loop fusion | bytes 8388612 | tf_op jit(solution)/shard_map/slice | solution.py:22
  43.4 0.0 copy-start
  43.4 0.4 bitcast_select_fusion
  43.8 0.9 copy-done
  44.8 2.4 %fusion.1 = f32[1024,4096]{1,0:T(8,128)S(1)} fusion(bf16[256,4096]{1,0:T(8,128)(2,1)S(1)} %bitcast_select_fusion, bf16[256,4096]{1,0:T(8,128)(2,1)S(1)} %bitcast.21, s32[]{:T(128)S(6)} %select_n.18), kind=kOutput, calls=%fused_computation.10 | convolution fusion | flops 2147483648 | bytes 19398660 | tf_op jit(solution)/shard_map/tr,ts->rs/dot_general | solution.py:33
  47.2 8.8 %fusion.11 = (f32[1024]{0:T(1024)S(1)}, f32[1024,4096]{1,0:T(8,128)}) fusion(f32[1024,4096]{1,0:T(8,128)S(1)} %fusion.1, bf16[256,4096]{1,0:T(8,128)(2,1)} %bitcast.22, bf16[256,4096]{1,0:T(8,128)(2,1)S(1)} %bitcast_select_fusion, s32[]{:T(128)S(6)} %select_n.18), kind=kOutput, calls=%fused_computation.31 | convolution fusion | flops 2155871232 | bytes 36179972 | tf_op jit(solution)/shard_map/tr,ts->rs/dot_general | solution.py:34
  56.0 5.2 %all_gather.28 = f32[4096]{0:T(1024)S(1)} all-gather(f32[1024]{0:T(1024)S(1)} %broadcast_multiply_fusion.1), channel_id=1, replica_groups=mesh['frames'=4,'win'=8] {'frames'}, dimensions={0}, use_global_device_ids=true | all-gather | bytes 20480 | tf_op jit(solution)/shard_map/all_gather | solution.py:61
  61.2 21.3 %psum.7 = f32[1024]{0:T(1024)S(1)} all-reduce(f32[1024]{0:T(1024)S(1)} %broadcast_multiply_fusion.1), channel_id=1, replica_groups=mesh['frames'=4,'win'=8] {'win'}, use_global_device_ids=true, to_apply=%region_1.2 | all-reduce | flops 1024 | bytes 8192 | tf_op jit(solution)/shard_map/psum | solution.py:63
  82.5 9.1 %multiply_reduce_fusion.2 = (f32[1024]{0:T(1024)S(1)}, f32[1024]{0:T(1024)S(1)}) fusion(f32[4096]{0:T(1024)S(1)} %all_gather.28, f32[4096]{0:T(1024)S(1)} %bitcast.26, f32[1024,4096]{1,0:T(8,128)} %get-tuple-element.11, f32[1024]{0:T(1024)S(1)} %dynamic-slice_multiply_fusion, f32[1024]{0:T(1024)S(1)} %broadcast_multiply_fusion.1), kind=kLoop, calls=%fused_computation.3 | loop fusion | flops 33552384 | bytes 16826368 | tf_op jit(solution)/shard_map/reduce_sum | solution.py:71
  91.7 5.2 %all_gather.32 = f32[4096]{0:T(1024)S(1)} all-gather(f32[1024]{0:T(1024)S(1)} %fusion.9), channel_id=1, replica_groups=mesh['frames'=4,'win'=8] {'frames'}, dimensions={0}, use_global_device_ids=true | all-gather | bytes 20480 | tf_op jit(solution)/shard_map/all_gather | solution.py:77
  96.9 30.6 %all-gather = f32[8192]{0:T(1024)S(1)} all-gather(f32[1024]{0:T(1024)S(1)} %mul.185), channel_id=2, replica_groups=mesh['frames'=4,'win'=8] {'win'}, dimensions={0}, use_global_device_ids=true | all-gather | bytes 36864 | tf_op jit(solution)/shard_map/all_gather | solution.py:72
  127.5 0.6 reduce_sum.99
  128.1 5.2 %all_gather.31 = f32[4096]{0:T(1024)S(1)} all-gather(f32[1024]{0:T(1024)S(1)} %div.38), channel_id=1, replica_groups=mesh['frames'=4,'win'=8] {'frames'}, dimensions={0}, use_global_device_ids=true | all-gather | bytes 20480 | tf_op jit(solution)/shard_map/all_gather | solution.py:76
  133.3 0.6 reduce_sum.94
  133.9 0.7 divide_multiply_fusion
  134.6 9.0 %multiply_reduce_fusion = (f32[1024]{0:T(1024)S(1)}, f32[1024]{0:T(1024)S(1)}) fusion(f32[4096]{0:T(1024)S(1)} %divide_multiply_fusion, f32[4096]{0:T(1024)S(1)} %all_gather.32, f32[1024,4096]{1,0:T(8,128)} %get-tuple-element.11, f32[1024]{0:T(1024)S(1)} %dynamic_slice.33, f32[1024]{0:T(1024)S(1)} %fusion.9), kind=kLoop, calls=%fused_computation | loop fusion | flops 33552384 | bytes 16826368 | tf_op jit(solution)/shard_map/reduce_sum | solution.py:70
  143.6 30.6 %all-gather.1 = f32[8192]{0:T(1024)S(1)} all-gather(f32[1024]{0:T(1024)S(1)} %mul.193), channel_id=3, replica_groups=mesh['frames'=4,'win'=8] {'win'}, dimensions={0}, use_global_device_ids=true | all-gather | bytes 36864 | tf_op jit(solution)/shard_map/all_gather | solution.py:72
  174.2 5.2 %all_gather.35 = f32[4096]{0:T(1024)S(1)} all-gather(f32[1024]{0:T(1024)S(1)} %div.42), channel_id=1, replica_groups=mesh['frames'=4,'win'=8] {'frames'}, dimensions={0}, use_global_device_ids=true | all-gather | bytes 20480 | tf_op jit(solution)/shard_map/all_gather | solution.py:80
  179.4 0.6 reduce_sum.97
  180.0 1.3 fusion.5
  181.3 1.2 divide_log_fusion
  (14 shorter events, 0.1 us)
Async XLA Ops:
  7.2 33.3 %all-gather.4.cloned.1.call-start = ((), (), s32[]{:S(2)}) async-start(), calls=%async_computation | async-start | bytes 2949120 | tf_op jit(solution)/shard_map/all_gather | solution.py:55
  8.5 3.1 %collective-permute-start = (bf16[8,4096]{1,0:T(8,128)(2,1)S(1)}, bf16[8,4096]{1,0:T(8,128)(2,1)S(1)}, u32[]{:S(2)}, u32[]{:S(2)}) collective-permute-start(bf16[8,4096]{1,0:T(8,128)(2,1)S(1)} %slice_bitcast_fusion), channel_id=1, source_target_pairs={{8,0},{16,8},{24,16},{9,1},{17,9},{25,17},{10,2},{18,10},{26,18},{... | collective-permute-start | bytes 196616 | tf_op jit(solution)/shard_map/ppermute | solution.py:14
  43.4 1.4 copy-start
Sparse Core Ops, SparseCore 0:
  12.7 27.7 all-gather.3
